TPU v7x, 32 devices: a whole 2x2x4 slice. The times are simulated.
32 devices in a mesh: runs: 2 (over y), gx: 4 (over z), gy: 2 (over core), gz: 2 (over x).
Axes of the slice: x: 2, y: 2, z: 4, core: 2. Of those that a mesh axis runs over, the one named last changes fastest.
Arguments:
- labels: int32 [24, 128, 1024], P(('runs', 'gz'), 'gx', 'gy'), parts along dimension 0, may hold values from 0 to 3
- background: bfloat16 [24, 128, 1024], P(('runs', 'gz'), 'gx', 'gy'), parts along dimension 0, may hold values from -3 to 3
- contrasts: float32 [8], P('runs'), parts along dimension 0, may hold values from -1 to 1
- kernels: bfloat16 [24, 15, 15], P(('runs', 'gz')), parts along dimension 0, may hold values from -0.125 to 0.125
- observed: float32 [6, 128, 1024], P('runs', 'gx', 'gy'), parts along dimension 0, may hold values from -6 to 6
Outputs:
- residual: float32 [6, 128, 1024], P('runs', ('gx', 'gz'), 'gy'), parts along dimension 0
- gradient: float32 [24, 128, 1024], P(('runs', 'gz'), 'gx', 'gy'), parts along dimension 0
There are 2 independent parts, one for each index of `runs`. A program takes and returns all parts, laid end to end along the dimension named above; each array names one. Nothing has to cross between parts.
All inputs are finite; a program needn't handle non-finite values.
Results may differ from a plain program's by a relative error of at most 0.0058.
Values may be sent and summed in bfloat16 or wider, within the bound.
No kernel may reach another device: no remote copies, remote signals or barrier semaphores. Data moves between devices by JAX's collectives and lax.ppermute only.
A program may use at most 64 MiB of HBM per device.

v0:
```python
import functools

import jax
import jax.numpy as jnp
from jax import lax
from jax.experimental import pallas as pl
from jax.experimental.pallas import tpu as pltpu
from jax.sharding import PartitionSpec as P


descent = 0.01
ITERS = 2
PART = 48
NEAR, HALO = 9, 25
FULL = 64
WIDE = 256
GRANT = 16 * 2**20

f32 = jnp.float32
bf16 = jnp.bfloat16


def iota(shape, dim):
    return lax.broadcasted_iota(jnp.int32, shape, dim)


def up_rows(v):
    return pltpu.roll(v, v.shape[0] - 1, 0)


def down_rows(v):
    return pltpu.roll(v, 1, 0)


def right(v):
    return pltpu.roll(v, v.shape[1] - 1, 1)


def left(v):
    return pltpu.roll(v, 1, 1)


def tensor_fields(s):
    above, below = up_rows(s), down_rows(s)
    along_x = above + below - 2.0 * s
    along_y = right(s) + left(s) - 2.0 * s
    diff = above - below
    mixed = 0.25 * (right(diff) - left(diff))
    return along_x, along_y, mixed


def adjoint_of(r0, r1, r2):
    cross = 0.25 * (right(r2) - left(r2))
    return (
        up_rows(r0 + cross)
        + down_rows(r0 - cross)
        - 2.0 * r0
        + right(r1)
        + left(r1)
        - 2.0 * r1
    )


def adjoint_square(s):
    def row(k):
        return pltpu.roll(s, -k % FULL, 0)[8 : 8 + PART]

    def column(v, k):
        return pltpu.roll(v, -k % v.shape[1], 1)

    centre = s[8 : 8 + PART]
    near, far = row(1) + row(-1), row(2) + row(-2)
    mixed = 0.0625 * (far - 2.0 * centre)
    both = centre + mixed
    return (
        (far - 4.0 * near + 12.0 * centre - 2.0 * mixed)
        + (column(both, 2) + column(both, -2))
        - 4.0 * (column(centre, 1) + column(centre, -1))
    )


def edge_columns(first, last, side=None):
    lane = iota(first.shape, 1)
    inside = jnp.where(lane < 64, pltpu.roll(first, 32, 1), last)
    if side is None:
        return jnp.where(lane < 32, jnp.zeros_like(first), inside)
    outside = jnp.where(lane < 16, side, pltpu.roll(side, 32, 1))
    return jnp.where(lane < 32, outside, inside)


def edges_of(v):
    width = v.shape[1]
    return edge_columns(v[:, :128], v[:, width - 256 : width - 128], v[:, width - 128 :])


def add_edges(field, message):
    width = field.shape[1]
    lane = iota(message.shape, 1)
    turned = pltpu.roll(message, 96, 1)
    zero = jnp.zeros_like(message)
    first = field[:, :128] + jnp.where(lane < NEAR, message, zero)
    last = field[:, width - 256 : width - 128] + jnp.where(lane >= 128 - NEAR, turned, zero)
    side = field[:, width - 128 :] + jnp.where(
        lane < HALO, turned, jnp.where(lane >= 128 - HALO, message, zero)
    )
    return jnp.concatenate([first, field[:, 128 : width - 256], last, side], axis=1)


def kernel_rows(k_ref, taps_ref):
    layers, span, _ = k_ref.shape
    taps_ref[...] = jnp.zeros(taps_ref.shape, f32)
    for l in range(layers):
        taps_ref[16 * l : 16 * l + span, :span] = k_ref[l].astype(f32)
    shape = (taps_ref.shape[0], WIDE)
    source = iota(shape, 0)
    place = jnp.where(32 * (source >> 4) + (source & 15) == iota(shape, 1), 1.0, 0.0)
    return lax.dot_general(
        taps_ref[...].astype(bf16),
        place.astype(bf16),
        (((0,), (0,)), ((), ())),
        preferred_element_type=f32,
    )


def build_bands(base_ref, bands_ref, span):
    tap = (iota((8, 128), 1) & 31) - iota((8, 128), 0) + 15
    keep = [(tap - 8 * g >= 0) & (tap - 8 * g < span) for g in range(PART // 8)]
    for block in range(WIDE // 128):
        for j in range(span):
            row = jnp.broadcast_to(
                base_ref[j : j + 1, 128 * block : 128 * block + 128], (8, 128)
            )
            moved = [
                jnp.where(
                    keep[g],
                    pltpu.roll(row, (8 * g - 15) % 128, 1, stride=1, stride_axis=0),
                    0.0,
                )
                for g in range(PART // 8)
            ]
            bands_ref[
                j * PART : (j + 1) * PART, 128 * block : 128 * block + 128
            ] = jnp.concatenate(moved, axis=0).astype(bf16)


def scatter_surface(bands, rounded, prod_ref, span, radius):
    width = rounded.shape[1]
    prod_ref[...] = jnp.dot(bands, rounded, preferred_element_type=f32)
    total = prod_ref[radius * PART : (radius + 1) * PART, :]
    for j in range(span):
        if j != radius:
            piece = prod_ref[j * PART : (j + 1) * PART, :]
            total = total + pltpu.roll(piece, (radius - j) % width, 1)
    return total


def fold_side(side, reach):
    lane = iota((8, 128), 1)
    used = (lane < reach) | (lane >= 128 - reach)
    count = 128 // (2 * reach)
    blocks = []
    for first in range(0, PART // 8, count):
        folded = jnp.zeros((8, 128), f32)
        for n, g in enumerate(range(first, min(first + count, PART // 8))):
            piece = jnp.where(used, side[8 * g : 8 * g + 8], 0.0)
            folded = folded + pltpu.roll(piece, reach + 2 * reach * n, 1)
        blocks.append(folded)
    return blocks


def unfold_side(blocks, reach):
    lane = iota((8, 128), 1)
    used = (lane < reach) | (lane >= 128 - reach)
    count = 128 // (2 * reach)
    pieces = []
    for g in range(PART // 8):
        piece = pltpu.roll(blocks[g // count], 128 - reach - 2 * reach * (g % count), 1)
        pieces.append(jnp.where(used, piece, 0.0))
    return jnp.concatenate(pieces, axis=0)


def depth_message_rows(cells_y, reach):
    blocks = -(-(PART // 8) // (128 // (2 * reach)))
    return PART * (cells_y // 128) + 8 * (blocks - 1)


def fold_places(cells_y):
    blocks = cells_y // 128
    return [PART * (n % blocks) + (PART - 1) * (n // blocks) for n in range(8)]


def store_depth_message(out_ref, part, cells_y, reach):
    for start in range(0, cells_y, 128):
        row = PART * (start // 128)
        out_ref[row : row + PART, :] = part[:, start : start + 128]
    folded, *others = fold_side(part[:, cells_y:], reach)
    for n, row in enumerate(fold_places(cells_y)):
        out_ref[row : row + 1, :] = folded[n : n + 1]
    for n, block in enumerate(others):
        row = PART * (cells_y // 128) + 8 * n
        out_ref[row : row + 8, :] = block


def first_kernel(
    labels_hbm, background_hbm, contrasts_hbm, k_hbm,
    out_ref, edge_ref, density_edge_ref, density_ref, bands_ref,
    labels_ref, background_ref, contrasts_ref, k_ref, sems,
    taps_ref, base_ref, prod_ref,
):
    layers, cells_x, cells_y = labels_ref.shape
    span = k_ref.shape[1]
    copies = [
        pltpu.make_async_copy(source, target, sems.at[n])
        for n, (source, target) in enumerate(
            (
                (k_hbm, k_ref),
                (contrasts_hbm, contrasts_ref),
                (labels_hbm, labels_ref),
                (background_hbm, background_ref),
            )
        )
    ]
    for copy in copies:
        copy.start()
    copies[0].wait()
    base_ref[...] = kernel_rows(k_ref, taps_ref)
    build_bands(base_ref, bands_ref, span)
    for copy in copies[1:]:
        copy.wait()
    classes = contrasts_ref.shape[0]
    for l in range(layers):
        label = labels_ref[l]
        value = jnp.full(label.shape, contrasts_ref[0], f32)
        for c in range(1, classes):
            value = jnp.where(label == c, contrasts_ref[c], value)
        density = value + background_ref[l].astype(f32)
        rows = slice(l * cells_x, (l + 1) * cells_x)
        density_ref[rows, :] = density
        density_edge_ref[rows, :] = edge_columns(
            density[:, :128], density[:, cells_y - 128 :]
        )
    lanes = layers * cells_x
    radius = (span - 1) // 2
    width = cells_y + 128
    prod_ref[...] = jnp.dot(
        bands_ref[:, :lanes], density_ref[...].astype(bf16), preferred_element_type=f32
    )
    part = jnp.zeros((PART, width), f32)
    side = jnp.zeros((PART, 128), f32)
    for j in range(span):
        piece = jnp.concatenate([prod_ref[j * PART : (j + 1) * PART, :], side], axis=1)
        shift = (radius - j) % width
        part = part + (pltpu.roll(piece, shift, 1) if shift else piece)
    edge_ref[...] = edges_of(part)
    store_depth_message(out_ref, part, cells_y, NEAR)


def observed_kernel(
    density_edge_ref, observed_hbm, q_ref, edge_ref, observed_ref, obs_ref, sem
):
    cells_y = observed_ref.shape[2]
    copy = pltpu.make_async_copy(observed_hbm, observed_ref, sem)
    copy.start()
    edge_ref[PART:, :] = density_edge_ref[...]
    obs_ref[...] = jnp.zeros(obs_ref.shape, f32)
    copy.wait()
    for k in range(3):
        obs_ref[k, 8 : PART - 8, :cells_y] = observed_ref[k]
    q = adjoint_of(obs_ref[0], obs_ref[1], obs_ref[2])
    q_ref[...] = q
    edge_ref[:PART, :] = edges_of(q)


def transpose_kernel(bands_ref, out_ref):
    out_ref[...] = bands_ref[...].astype(f32).T.astype(bf16)


def rows_kernel(
    part_ref, other_ref, edge_ref, edge_other_ref, q_ref, q_edge_ref,
    sum_ref, up_ref, down_ref, q_out_ref,
    dense_ref, fold_ref,
):
    cells_y = sum_ref.shape[1] - 128
    dense_ref[...] = part_ref[...] + other_ref[...]
    zero = jnp.zeros((1, 128), f32)
    for n, row in enumerate(fold_places(cells_y)):
        fold_ref[n : n + 1, :] = dense_ref[row : row + 1, :]
    folded = [fold_ref[...]]
    for row in range(PART * (cells_y // 128), dense_ref.shape[0], 8):
        folded.append(dense_ref[row : row + 8, :])
    for row in fold_places(cells_y):
        dense_ref[row : row + 1, :] = zero
    for start in range(0, cells_y, 128):
        row = PART * (start // 128)
        sum_ref[:, start : start + 128] = dense_ref[row : row + PART, :]
    sum_ref[:, cells_y:] = unfold_side(folded, NEAR)
    if edge_ref is not None:
        sum_ref[...] = add_edges(sum_ref[...], edge_ref[...] + edge_other_ref[...])
    sub = iota((8, sum_ref.shape[1]), 0)
    up_ref[:8, :] = sum_ref[8:16, :]
    up_ref[8:16, :] = jnp.where(sub >= 1, sum_ref[:8, :], sum_ref[16:24, :])
    down_ref[:8, :] = sum_ref[32:40, :]
    down_ref[8:16, :] = jnp.where(sub < 7, sum_ref[40:48, :], sum_ref[24:32, :])
    if q_ref is not None:
        q_out_ref[...] = add_edges(q_ref[...], q_edge_ref[:PART, :])
        up_ref[16:24, :] = jnp.where(sub < 7, q_out_ref[8:16, :], q_out_ref[:8, :])
        down_ref[16:24, :] = jnp.where(sub >= 1, q_out_ref[32:40, :], q_out_ref[40:48, :])


def full_surface(total, above, below):
    shape = (8, total.shape[1])
    sub = iota(shape, 0)
    zero = jnp.zeros(shape, f32)
    return jnp.concatenate(
        [
            jnp.where(sub == 7, above[8:16], zero),
            total[:8] + above[:8],
            total[8:16] + jnp.where(sub < 7, above[8:16], zero),
            total[16:32],
            total[32:40] + jnp.where(sub >= 1, below[8:16], zero),
            total[40:48] + below[:8],
            jnp.where(sub == 0, below[8:16], zero),
        ],
        axis=0,
    )


def full_q(q, above, below):
    shape = (8, q.shape[1])
    sub = iota(shape, 0)
    zero = jnp.zeros(shape, f32)
    return jnp.concatenate(
        [
            q[:8] + jnp.where(sub >= 1, above[16:24], zero),
            q[8:16] + jnp.where(sub == 0, above[16:24], zero),
            q[16:32],
            q[32:40] + jnp.where(sub == 7, below[16:24], zero),
            q[40:48] + jnp.where(sub < 7, below[16:24], zero),
        ],
        axis=0,
    )


def stack_shifts(adjoint, stack_ref, columns, span, radius):
    for j in range(span):
        shift = (j - radius) % adjoint.shape[1]
        moved = pltpu.roll(adjoint, shift, 1) if shift else adjoint
        stack_ref[j * PART : (j + 1) * PART, columns] = moved[:, columns]


def rounded_adjoint(s, q):
    return (adjoint_square(s) - q).astype(bf16)


def middle_kernel(
    sum_ref, above_ref, below_ref, q_ref, density_ref, edge_ref, bands_ref, turned_ref,
    out_ref, q_out_ref,
    stack_ref, prod_ref, *, span,
):
    radius = (span - 1) // 2
    lanes, cells_y = density_ref.shape
    above, below = above_ref[...], below_ref[...]
    q = full_q(q_ref[...], above, below)
    q_out_ref[...] = q
    adjoint = rounded_adjoint(full_surface(sum_ref[...], above, below), q)
    stack_shifts(adjoint, stack_ref, slice(0, cells_y + 128), span, radius)
    gradient = jnp.dot(turned_ref[:lanes, :], stack_ref[...], preferred_element_type=f32)
    density = density_ref[...] - descent * gradient[:, :cells_y]
    message = edge_ref[PART:, :]
    lane = iota(message.shape, 1)
    outside = jnp.where(lane < 16, pltpu.roll(message, 96, 1), message)
    outside = outside - descent * gradient[:, cells_y:]
    outside = jnp.where((lane < 16) | (lane >= 112), outside, 0.0)
    rounded = jnp.concatenate([density.astype(bf16), outside.astype(bf16)], axis=1)
    part = scatter_surface(bands_ref[:, :lanes], rounded, prod_ref, span, radius)
    store_depth_message(out_ref, part, cells_y, NEAR)


def last_kernel(
    sum_ref, above_ref, below_ref, q_ref, turned_ref, observed_ref,
    residual_hbm, gradient_hbm,
    residual_ref, gradient_ref, sems, full_ref, stack_ref, misfit_ref, *, span,
):
    radius = (span - 1) // 2
    layers, cells_x, cells_y = gradient_ref.shape
    s = full_surface(sum_ref[...], above_ref[...], below_ref[...])
    full_ref[...] = s
    adjoint = rounded_adjoint(s, q_ref[...])
    turned = turned_ref[: layers * cells_x, :]
    half = cells_y // 2
    copies = []
    for n in range(2):
        columns = slice(n * half, (n + 1) * half)
        stack_shifts(adjoint, stack_ref, columns, span, radius)
        gradient = jnp.dot(turned, stack_ref[:, columns], preferred_element_type=f32)
        for l in range(layers):
            gradient_ref[l, :, columns] = gradient[l * cells_x : (l + 1) * cells_x, :]
        copies.append(
            pltpu.make_async_copy(
                gradient_ref.at[:, :, columns], gradient_hbm.at[:, :, columns], sems.at[n]
            )
        )
        copies[-1].start()
    share = residual_ref.shape[1]
    if share % 8 == 0:
        start = pl.multiple_of(lax.axis_index("gz") * share, 8)
        fields = tensor_fields(full_ref[pl.ds(start + 8, share + 16), :])
        for k in range(3):
            residual_ref[k] = (
                fields[k][8 : 8 + share, :cells_y] - observed_ref[k, pl.ds(start, share), :]
            )
    else:
        fields = tensor_fields(full_ref[...])
        for k in range(3):
            misfit_ref[k] = fields[k][16 : 16 + cells_x, :cells_y] - observed_ref[k]
        for start in range(0, cells_x, share):

            @pl.when(lax.axis_index("gz") * share == start)
            def _():
                residual_ref[...] = misfit_ref[:, start : start + share, :]

    copies.append(pltpu.make_async_copy(residual_ref, residual_hbm, sems.at[2]))
    copies[-1].start()
    for copy in copies:
        copy.wait()


def call(kernel, outs, scratch=(), inputs=None, results=pltpu.VMEM):
    made = pl.BlockSpec(memory_space=results)

    def run(*operands):
        spaces = inputs or (pltpu.VMEM,) * len(operands)
        operands = [
            pltpu.with_memory_space_constraint(v, space) if space is pltpu.HBM else v
            for v, space in zip(operands, spaces)
        ]
        return pl.pallas_call(
            kernel,
            out_shape=outs,
            in_specs=[pl.BlockSpec(memory_space=space) for space in spaces],
            out_specs=jax.tree.map(lambda _: made, outs),
            scratch_shapes=[
                pltpu.VMEM(*item) if isinstance(item, tuple) else item for item in scratch
            ],
            compiler_params=pltpu.CompilerParams(vmem_limit_bytes=GRANT),
        )(*operands)

    return run


def shaped(shape, kind=f32):
    return jax.ShapeDtypeStruct(shape, kind)


def swap(value, axis, distance):
    peers = lax.axis_size(axis)
    return lax.ppermute(value, axis, [(i, i ^ distance) for i in range(peers)])


def body(labels, background, contrasts, kernels, observed):
    layers, cells_x, cells_y = labels.shape
    span = kernels.shape[1]
    lanes = layers * cells_x
    width = cells_y + 128
    depth_peers, row_peers = lax.axis_size("gz"), lax.axis_size("gx")
    assert cells_x == 32 and span == 15 and lanes <= 192 and cells_y == 512 and lax.axis_size("gy") == 2
    assert depth_peers & (depth_peers - 1) == 0
    share = cells_x // depth_peers
    upward = [(i, (i - 1) % row_peers) for i in range(row_peers)]
    downward = [(j, i) for i, j in upward]
    full = ((FULL, width), f32)
    prod = ((span * PART, cells_y), f32)
    field = shaped((PART, width))

    def kernel_of(body_of):
        return functools.partial(body_of, span=span)

    message = shaped((depth_message_rows(cells_y, NEAR), 128))
    part, edge, density_edge, density, bands = call(
        first_kernel,
        (
            message,
            shaped((PART, 128)),
            shaped((lanes, 128)),
            shaped((lanes, cells_y)),
            shaped((span * PART, WIDE), bf16),
        ),
        (
            (labels.shape, labels.dtype),
            (background.shape, background.dtype),
            pltpu.SMEM(contrasts.shape, contrasts.dtype),
            (kernels.shape, kernels.dtype),
            pltpu.SemaphoreType.DMA((4,)),
            ((16 * layers, 16), f32),
            ((16, WIDE), f32),
            prod,
        ),
        inputs=(pltpu.HBM,) * 4,
    )(labels, background, contrasts, kernels)
    turned = call(transpose_kernel, shaped((WIDE, span * PART), bf16))(bands)

    distances = [2 << bit for bit in range(depth_peers.bit_length() - 2)] + [1]
    for iteration in range(ITERS):
        scratch = ((part.shape, f32), ((8, 128), f32))
        if iteration == 0:
            other = swap(part, "gz", distances[0])
            edge = swap(edge, "gy", 1)
            edge, density_edge = lax.optimization_barrier((edge, density_edge))
            edge_other = swap(edge, "gz", distances[0])
            q, q_edge, observed = call(
                observed_kernel,
                (field, shaped((PART + lanes, 128)), shaped(observed.shape)),
                (((3, PART, width), f32), pltpu.SemaphoreType.DMA),
                inputs=(pltpu.VMEM, pltpu.HBM),
            )(density_edge, observed)
            others = swap(q_edge, "gy", 1)
            for distance in distances[1:]:
                part, edge = part + other, edge + edge_other
                other = swap(part, "gz", distance)
                edge_other = swap(edge, "gz", distance)
        else:
            for distance in distances[:-1]:
                part = part + swap(part, "gz", distance)
            other = swap(part, "gz", 1)
        if iteration == 0:
            total, up, down, q = call(
                rows_kernel,
                (field, shaped((24, width)), shaped((24, width)), field),
                scratch,
            )(part, other, edge, edge_other, q, others)
        else:
            total, up, down = call(
                lambda a, b, c, d, e, f, g: rows_kernel(
                    a, b, None, None, None, None, c, d, e, None, f, g
                ),
                (field, shaped((16, width)), shaped((16, width))),
                scratch,
            )(part, other)
        below = lax.ppermute(up, "gx", upward)
        above = lax.ppermute(down, "gx", downward)
        if iteration == 0:
            part, q = call(
                kernel_of(middle_kernel),
                (shaped((depth_message_rows(cells_y, NEAR), 128)), field),
                (((span * PART, width), bf16), ((span * PART, width), f32)),
            )(total, above, below, q, density, others, bands, turned)
    return call(
        kernel_of(last_kernel),
        (shaped((3, share, cells_y)), shaped((layers, cells_x, cells_y))),
        (
            ((3, share, cells_y), f32),
            ((layers, cells_x, cells_y), f32),
            pltpu.SemaphoreType.DMA((3,)),
            full,
            ((span * PART, cells_y), bf16),
            ((3, cells_x, cells_y), f32),
        ),
        results=pltpu.HBM,
    )(total, above, below, q, turned, observed)


def solution(mesh):
    placed = (
        P(("runs", "gz"), "gx", "gy"),
        P(("runs", "gz"), "gx", "gy"),
        P("runs"),
        P(("runs", "gz"), None, None),
        P("runs", "gx", "gy"),
    )
    return jax.shard_map(
        body,
        mesh=mesh,
        in_specs=placed,
        out_specs=(P("runs", ("gx", "gz"), "gy"), P(("runs", "gz"), "gx", "gy")),
        check_vma=False,
    )
```

profile of v0, /device:TPU:0, one launch (start us, length us, event | category | flops | bytes accessed | tf_op | source)
XLA Modules:
  0.0 32.3 jit_solution(18188032314243632297)
XLA Ops:
  0.6 1.9 %shard_map.68 = (f32[192,128]{1,0:T(8,128)S(1)}, f32[48,128]{1,0:T(8,128)S(1)}, f32[192,128]{1,0:T(8,128)S(1)}, f32[192,512]{1,0:T(8,128)S(1)}, bf16[720,256]{1,0:T(8,128)(2,1)S(1)}) custom-call(s32[6,32,512]{2,1,0:T(8,128)} %labels_hbm.1, bf16[6,32,512]{2,1,0:T(8,128)(2,1)} %background_hbm.1, f32[4]{0:T(128)} %contrasts_hbm.1, bf16[6,15,15]{2,1,0:T(8,128)(2,1)} %k_hbm.1), custom_call_target="tpu_custom_call" | custom-call | tf_op jit(solution)/shard_map/pallas_call | solution.py:437
  2.5 0.6 %collective-permute-start.1 = (f32[48,128]{1,0:T(8,128)S(1)}, f32[48,128]{1,0:T(8,128)S(1)}, u32[]{:S(2)}, u32[]{:S(2)}) collective-permute-start(f32[48,128]{1,0:T(8,128)S(1)} %get-tuple-element.22), channel_id=1, source_target_pairs={{0,2},{2,0},{1,3},{3,1},{4,6},{6,4},{5,7},{7,5},{8,10},{10,8},{9,1... | collective-permute-start | bytes 73736 | tf_op jit(solution)/shard_map/ppermute | solution.py:457
  3.1 0.8 %collective-permute-done.1.edge_ref = f32[48,128]{1,0:T(8,128)S(1)} collective-permute-done((f32[48,128]{1,0:T(8,128)S(1)}, f32[48,128]{1,0:T(8,128)S(1)}, u32[]{:S(2)}, u32[]{:S(2)}) %collective-permute-start.1) | collective-permute-done | bytes 24608 | tf_op jit(solution)/shard_map/ppermute | solution.py:457
  3.9 1.2 %shard_map.69 = (f32[48,640]{1,0:T(8,128)S(1)}, f32[240,128]{1,0:T(8,128)S(1)}, f32[3,32,512]{2,1,0:T(8,128)S(1)}) custom-call(f32[192,128]{1,0:T(8,128)S(1)} %get-tuple-element.25.density_edge_ref, f32[3,32,512]{2,1,0:T(8,128)} %observed_hbm.1), custom_call_target="tpu_custom_call" | custom-call | tf_op jit(solution)/shard_map/pallas_call | solution.py:437
  5.1 0.4 %collective-permute-start.3 = (f32[240,128]{1,0:T(8,128)S(1)}, f32[240,128]{1,0:T(8,128)S(1)}, u32[]{:S(2)}, u32[]{:S(2)}) collective-permute-start(f32[240,128]{1,0:T(8,128)S(1)} %get-tuple-element.27), channel_id=1, source_target_pairs={{0,2},{2,0},{1,3},{3,1},{4,6},{6,4},{5,7},{7,5},{8,10},{10,8},{9,1... | collective-permute-start | bytes 368648 | tf_op jit(solution)/shard_map/ppermute | solution.py:457
  5.5 2.6 %collective-permute-start = (f32[192,128]{1,0:T(8,128)S(1)}, f32[192,128]{1,0:T(8,128)S(1)}, u32[]{:S(2)}, u32[]{:S(2)}) collective-permute-start(f32[192,128]{1,0:T(8,128)S(1)} %get-tuple-element.21.part_ref), channel_id=1, source_target_pairs={{0,1},{1,0},{2,3},{3,2},{4,5},{5,4},{6,7},{7,6},{8,9},{9,8},{10,11... | collective-permute-start | bytes 294920 | tf_op jit(solution)/shard_map/ppermute | solution.py:457
  8.2 0.0 collective-permute-start.2
  8.2 3.8 %collective-permute-done.2.edge_other_ref = f32[48,128]{1,0:T(8,128)S(1)} collective-permute-done((f32[48,128]{1,0:T(8,128)S(1)}, f32[48,128]{1,0:T(8,128)S(1)}, u32[]{:S(2)}, u32[]{:S(2)}) %collective-permute-start.2) | collective-permute-done | bytes 24608 | tf_op jit(solution)/shard_map/ppermute | solution.py:457
  12.0 0.0 collective-permute-done.other_ref
  12.0 0.0 collective-permute-done.3.q_edge_ref.edge_ref
  12.0 0.1 shard_map.70
  12.1 1.9 %collective-permute-start.4 = (f32[24,640]{1,0:T(8,128)S(1)}, f32[24,640]{1,0:T(8,128)S(1)}, u32[]{:S(2)}, u32[]{:S(2)}) collective-permute-start(f32[24,640]{1,0:T(8,128)S(1)} %get-tuple-element.29), channel_id=1, source_target_pairs={{12,0},{0,4},{4,8},{8,12},{13,1},{1,5},{5,9},{9,13},{14,2},{2,6},{... | collective-permute-start | bytes 184328 | tf_op jit(solution)/shard_map/ppermute | solution.py:540
  14.0 2.1 %collective-permute-start.5 = (f32[24,640]{1,0:T(8,128)S(1)}, f32[24,640]{1,0:T(8,128)S(1)}, u32[]{:S(2)}, u32[]{:S(2)}) collective-permute-start(f32[24,640]{1,0:T(8,128)S(1)} %get-tuple-element.30), channel_id=1, source_target_pairs={{0,12},{4,0},{8,4},{12,8},{1,13},{5,1},{9,5},{13,9},{2,14},{6,2},{... | collective-permute-start | bytes 184328 | tf_op jit(solution)/shard_map/ppermute | solution.py:539
  16.1 0.2 shard_map.71.turned_ref
  16.3 2.4 %collective-permute-done.4.above_ref = f32[24,640]{1,0:T(8,128)S(1)} collective-permute-done((f32[24,640]{1,0:T(8,128)S(1)}, f32[24,640]{1,0:T(8,128)S(1)}, u32[]{:S(2)}, u32[]{:S(2)}) %collective-permute-start.4) | collective-permute-done | bytes 61472 | tf_op jit(solution)/shard_map/ppermute | solution.py:540
  18.6 0.3 collective-permute-done.5.below_ref
  18.9 1.4 %shard_map.72 = (f32[192,128]{1,0:T(8,128)S(1)}, f32[48,640]{1,0:T(8,128)S(1)}) custom-call(f32[48,640]{1,0:T(8,128)S(1)} %get-tuple-element.28.sum_ref, f32[24,640]{1,0:T(8,128)S(1)} %collective-permute-done.4.above_ref, f32[24,640]{1,0:T(8,128)S(1)} %collective-permute-done.5.below_ref, f32[48,640]{1,0:T(8,128)S(1)} %get-tuple-element.31.q_ref, ...), custom_call_target="tpu_custom_call" | custom-call | tf_op jit(solution)/shard_map/pallas_call | solution.py:437
  20.2 1.7 %collective-permute-start.6 = (f32[192,128]{1,0:T(8,128)S(1)}, f32[192,128]{1,0:T(8,128)S(1)}, u32[]{:S(2)}, u32[]{:S(2)}) collective-permute-start(f32[192,128]{1,0:T(8,128)S(1)} %get-tuple-element.34.a), channel_id=1, source_target_pairs={{0,1},{1,0},{2,3},{3,2},{4,5},{5,4},{6,7},{7,6},{8,9},{9,8},{10,11... | collective-permute-start | bytes 294920 | tf_op jit(solution)/shard_map/ppermute | solution.py:457
  21.9 3.0 %collective-permute-done.6.b = f32[192,128]{1,0:T(8,128)S(1)} collective-permute-done((f32[192,128]{1,0:T(8,128)S(1)}, f32[192,128]{1,0:T(8,128)S(1)}, u32[]{:S(2)}, u32[]{:S(2)}) %collective-permute-start.6) | collective-permute-done | bytes 98336 | tf_op jit(solution)/shard_map/ppermute | solution.py:457
  24.9 0.1 shard_map.73
  25.0 0.9 %collective-permute-start.7 = (f32[16,640]{1,0:T(8,128)S(1)}, f32[16,640]{1,0:T(8,128)S(1)}, u32[]{:S(2)}, u32[]{:S(2)}) collective-permute-start(f32[16,640]{1,0:T(8,128)S(1)} %get-tuple-element.36), channel_id=1, source_target_pairs={{12,0},{0,4},{4,8},{8,12},{13,1},{1,5},{5,9},{9,13},{14,2},{2,6},{... | collective-permute-start | bytes 122888 | tf_op jit(solution)/shard_map/ppermute | solution.py:540
  25.9 2.9 %collective-permute-start.8 = (f32[16,640]{1,0:T(8,128)S(1)}, f32[16,640]{1,0:T(8,128)S(1)}, u32[]{:S(2)}, u32[]{:S(2)}) collective-permute-start(f32[16,640]{1,0:T(8,128)S(1)} %get-tuple-element.37), channel_id=1, source_target_pairs={{0,12},{4,0},{8,4},{12,8},{1,13},{5,1},{9,5},{13,9},{2,14},{6,2},{... | collective-permute-start | bytes 122888 | tf_op jit(solution)/shard_map/ppermute | solution.py:539
  28.8 2.0 %collective-permute-done.7.above_ref = f32[16,640]{1,0:T(8,128)S(1)} collective-permute-done((f32[16,640]{1,0:T(8,128)S(1)}, f32[16,640]{1,0:T(8,128)S(1)}, u32[]{:S(2)}, u32[]{:S(2)}) %collective-permute-start.7) | collective-permute-done | bytes 40992 | tf_op jit(solution)/shard_map/ppermute | solution.py:540
  30.8 1.5 %shard_map.74 = (f32[3,16,512]{2,1,0:T(8,128)}, f32[6,32,512]{2,1,0:T(8,128)}) custom-call(f32[48,640]{1,0:T(8,128)S(1)} %get-tuple-element.35.sum_ref, f32[16,640]{1,0:T(8,128)S(1)} %collective-permute-done.7.above_ref, f32[16,640]{1,0:T(8,128)S(1)} %collective-permute-done.8.below_ref, f32[48,640]{1,0:T(8,128)S(1)} %get-tuple-element.38.q_ref, ...), custom_call_target="tpu_custom_call" | custom-call | tf_op jit(solution)/shard_map/pallas_call | solution.py:437
  (1 shorter events, 0.0 us)
Async XLA Ops:
  2.5 1.4 %collective-permute-start.1 = (f32[48,128]{1,0:T(8,128)S(1)}, f32[48,128]{1,0:T(8,128)S(1)}, u32[]{:S(2)}, u32[]{:S(2)}) collective-permute-start(f32[48,128]{1,0:T(8,128)S(1)} %get-tuple-element.22), channel_id=1, source_target_pairs={{0,2},{2,0},{1,3},{3,1},{4,6},{6,4},{5,7},{7,5},{8,10},{10,8},{9,1... | collective-permute-start | bytes 73736 | tf_op jit(solution)/shard_map/ppermute | solution.py:457
  5.1 6.9 %collective-permute-start.3 = (f32[240,128]{1,0:T(8,128)S(1)}, f32[240,128]{1,0:T(8,128)S(1)}, u32[]{:S(2)}, u32[]{:S(2)}) collective-permute-start(f32[240,128]{1,0:T(8,128)S(1)} %get-tuple-element.27), channel_id=1, source_target_pairs={{0,2},{2,0},{1,3},{3,1},{4,6},{6,4},{5,7},{7,5},{8,10},{10,8},{9,1... | collective-permute-start | bytes 368648 | tf_op jit(solution)/shard_map/ppermute | solution.py:457
  5.5 6.5 %collective-permute-start = (f32[192,128]{1,0:T(8,128)S(1)}, f32[192,128]{1,0:T(8,128)S(1)}, u32[]{:S(2)}, u32[]{:S(2)}) collective-permute-start(f32[192,128]{1,0:T(8,128)S(1)} %get-tuple-element.21.part_ref), channel_id=1, source_target_pairs={{0,1},{1,0},{2,3},{3,2},{4,5},{5,4},{6,7},{7,6},{8,9},{9,8},{10,11... | collective-permute-start | bytes 294920 | tf_op jit(solution)/shard_map/ppermute | solution.py:457
  8.2 3.8 %collective-permute-start.2 = (f32[48,128]{1,0:T(8,128)S(1)}, f32[48,128]{1,0:T(8,128)S(1)}, u32[]{:S(2)}, u32[]{:S(2)}) collective-permute-start(f32[48,128]{1,0:T(8,128)S(1)} %collective-permute-done.1.edge_ref), channel_id=1, source_target_pairs={{0,1},{1,0},{2,3},{3,2},{4,5},{5,4},{6,7},{7,6},{8,9},{9,8},{10,11... | collective-permute-start | bytes 73736 | tf_op jit(solution)/shard_map/ppermute | solution.py:457
  12.1 6.5 %collective-permute-start.4 = (f32[24,640]{1,0:T(8,128)S(1)}, f32[24,640]{1,0:T(8,128)S(1)}, u32[]{:S(2)}, u32[]{:S(2)}) collective-permute-start(f32[24,640]{1,0:T(8,128)S(1)} %get-tuple-element.29), channel_id=1, source_target_pairs={{12,0},{0,4},{4,8},{8,12},{13,1},{1,5},{5,9},{9,13},{14,2},{2,6},{... | collective-permute-start | bytes 184328 | tf_op jit(solution)/shard_map/ppermute | solution.py:540
  14.0 4.9 %collective-permute-start.5 = (f32[24,640]{1,0:T(8,128)S(1)}, f32[24,640]{1,0:T(8,128)S(1)}, u32[]{:S(2)}, u32[]{:S(2)}) collective-permute-start(f32[24,640]{1,0:T(8,128)S(1)} %get-tuple-element.30), channel_id=1, source_target_pairs={{0,12},{4,0},{8,4},{12,8},{1,13},{5,1},{9,5},{13,9},{2,14},{6,2},{... | collective-permute-start | bytes 184328 | tf_op jit(solution)/shard_map/ppermute | solution.py:539
  20.2 4.7 %collective-permute-start.6 = (f32[192,128]{1,0:T(8,128)S(1)}, f32[192,128]{1,0:T(8,128)S(1)}, u32[]{:S(2)}, u32[]{:S(2)}) collective-permute-start(f32[192,128]{1,0:T(8,128)S(1)} %get-tuple-element.34.a), channel_id=1, source_target_pairs={{0,1},{1,0},{2,3},{3,2},{4,5},{5,4},{6,7},{7,6},{8,9},{9,8},{10,11... | collective-permute-start | bytes 294920 | tf_op jit(solution)/shard_map/ppermute | solution.py:457
  25.0 5.8 %collective-permute-start.7 = (f32[16,640]{1,0:T(8,128)S(1)}, f32[16,640]{1,0:T(8,128)S(1)}, u32[]{:S(2)}, u32[]{:S(2)}) collective-permute-start(f32[16,640]{1,0:T(8,128)S(1)} %get-tuple-element.36), channel_id=1, source_target_pairs={{12,0},{0,4},{4,8},{8,12},{13,1},{1,5},{5,9},{9,13},{14,2},{2,6},{... | collective-permute-start | bytes 122888 | tf_op jit(solution)/shard_map/ppermute | solution.py:540
  25.9 4.9 %collective-permute-start.8 = (f32[16,640]{1,0:T(8,128)S(1)}, f32[16,640]{1,0:T(8,128)S(1)}, u32[]{:S(2)}, u32[]{:S(2)}) collective-permute-start(f32[16,640]{1,0:T(8,128)S(1)} %get-tuple-element.37), channel_id=1, source_target_pairs={{0,12},{4,0},{8,4},{12,8},{1,13},{5,1},{9,5},{13,9},{2,14},{6,2},{... | collective-permute-start | bytes 122888 | tf_op jit(solution)/shard_map/ppermute | solution.py:539
where the time goes:
time: 32.5 us; the launch traced here: 32.3 us
  starting transfers between devices  13.1 us (40%)
  waiting for transfers between devices  12.2 us (38%)
  Pallas kernels  6.31 us (19%)
  between operations  0.67 us (2%)
    ppermute x5, waiting for transfers between devices, swap(): return lax.ppermute(value, axis, [(i, i ^ distance) for i in range(peers)])  7.61 us
    pallas_call x7, Pallas kernels, run(): pl.pallas_call(kernel, out_shape=outs, in_specs=[pl.BlockSpec(memory_spac...  6.31 us
    ppermute x5, starting transfers between devices, swap(): return lax.ppermute(value, axis, [(i, i ^ distance) for i in range(peers)])  5.34 us
    ppermute x2, starting transfers between devices, body(): below = lax.ppermute(up, 'gx', upward)  4.97 us
    ppermute x2, waiting for transfers between devices, body(): above = lax.ppermute(down, 'gx', downward)  4.37 us
    ppermute x2, starting transfers between devices, body(): above = lax.ppermute(down, 'gx', downward)  2.82 us
  transfers between devices with their start and end apart: 9, of which 6 were waited for; matrix products, arithmetic and copies ran while one was open for 0% of the time, Pallas kernels for 1%

commit v1 on v0

--- a/solution.py
+++ b/solution.py
@@ -395,12 +395,8 @@
         gradient = jnp.dot(turned, stack_ref[:, columns], preferred_element_type=f32)
         for l in range(layers):
             gradient_ref[l, :, columns] = gradient[l * cells_x : (l + 1) * cells_x, :]
-        copies.append(
-            pltpu.make_async_copy(
-                gradient_ref.at[:, :, columns], gradient_hbm.at[:, :, columns], sems.at[n]
-            )
-        )
-        copies[-1].start()
+    copies.append(pltpu.make_async_copy(gradient_ref, gradient_hbm, sems.at[0]))
+    copies[-1].start()
     share = residual_ref.shape[1]
     if share % 8 == 0:
         start = pl.multiple_of(lax.axis_index("gz") * share, 8)

time: 32.5 us -> 32.5 us (level)
  no operation moved by 1% of the time
where the time goes in v1:
time: 32.5 us; the launch traced here: 32.4 us
  starting transfers between devices  13.1 us (40%)
  waiting for transfers between devices  12.2 us (38%)
  Pallas kernels  6.31 us (19%)
  between operations  0.67 us (2%)
    ppermute x5, waiting for transfers between devices, swap(): return lax.ppermute(value, axis, [(i, i ^ distance) for i in range(peers)])  7.61 us
    pallas_call x7, Pallas kernels, run(): pl.pallas_call(kernel, out_shape=outs, in_specs=[pl.BlockSpec(memory_spac...  6.31 us
    ppermute x5, starting transfers between devices, swap(): return lax.ppermute(value, axis, [(i, i ^ distance) for i in range(peers)])  5.34 us
    ppermute x2, starting transfers between devices, body(): below = lax.ppermute(up, 'gx', upward)  4.97 us
    ppermute x2, waiting for transfers between devices, body(): above = lax.ppermute(down, 'gx', downward)  4.37 us
    ppermute x2, starting transfers between devices, body(): above = lax.ppermute(down, 'gx', downward)  2.82 us
  transfers between devices with their start and end apart: 9, of which 6 were waited for; matrix products, arithmetic and copies ran while one was open for 0% of the time, Pallas kernels for 1%

profile of v1, /device:TPU:0, one launch (start us, length us, event | category | flops | bytes accessed | tf_op | source)
XLA Modules:
  0.0 32.4 jit_solution(5339930410689191997)
XLA Ops:
  0.6 1.9 %shard_map.68 = (f32[192,128]{1,0:T(8,128)S(1)}, f32[48,128]{1,0:T(8,128)S(1)}, f32[192,128]{1,0:T(8,128)S(1)}, f32[192,512]{1,0:T(8,128)S(1)}, bf16[720,256]{1,0:T(8,128)(2,1)S(1)}) custom-call(s32[6,32,512]{2,1,0:T(8,128)} %labels_hbm.1, bf16[6,32,512]{2,1,0:T(8,128)(2,1)} %background_hbm.1, f32[4]{0:T(128)} %contrasts_hbm.1, bf16[6,15,15]{2,1,0:T(8,128)(2,1)} %k_hbm.1), custom_call_target="tpu_custom_call" | custom-call | tf_op jit(solution)/shard_map/pallas_call | solution.py:433
  2.5 0.6 %collective-permute-start.1 = (f32[48,128]{1,0:T(8,128)S(1)}, f32[48,128]{1,0:T(8,128)S(1)}, u32[]{:S(2)}, u32[]{:S(2)}) collective-permute-start(f32[48,128]{1,0:T(8,128)S(1)} %get-tuple-element.22), channel_id=1, source_target_pairs={{0,2},{2,0},{1,3},{3,1},{4,6},{6,4},{5,7},{7,5},{8,10},{10,8},{9,1... | collective-permute-start | bytes 73736 | tf_op jit(solution)/shard_map/ppermute | solution.py:453
  3.1 0.8 %collective-permute-done.1.edge_ref = f32[48,128]{1,0:T(8,128)S(1)} collective-permute-done((f32[48,128]{1,0:T(8,128)S(1)}, f32[48,128]{1,0:T(8,128)S(1)}, u32[]{:S(2)}, u32[]{:S(2)}) %collective-permute-start.1) | collective-permute-done | bytes 24608 | tf_op jit(solution)/shard_map/ppermute | solution.py:453
  3.9 1.2 %shard_map.69 = (f32[48,640]{1,0:T(8,128)S(1)}, f32[240,128]{1,0:T(8,128)S(1)}, f32[3,32,512]{2,1,0:T(8,128)S(1)}) custom-call(f32[192,128]{1,0:T(8,128)S(1)} %get-tuple-element.25.density_edge_ref, f32[3,32,512]{2,1,0:T(8,128)} %observed_hbm.1), custom_call_target="tpu_custom_call" | custom-call | tf_op jit(solution)/shard_map/pallas_call | solution.py:433
  5.1 0.4 %collective-permute-start.3 = (f32[240,128]{1,0:T(8,128)S(1)}, f32[240,128]{1,0:T(8,128)S(1)}, u32[]{:S(2)}, u32[]{:S(2)}) collective-permute-start(f32[240,128]{1,0:T(8,128)S(1)} %get-tuple-element.27), channel_id=1, source_target_pairs={{0,2},{2,0},{1,3},{3,1},{4,6},{6,4},{5,7},{7,5},{8,10},{10,8},{9,1... | collective-permute-start | bytes 368648 | tf_op jit(solution)/shard_map/ppermute | solution.py:453
  5.5 2.6 %collective-permute-start = (f32[192,128]{1,0:T(8,128)S(1)}, f32[192,128]{1,0:T(8,128)S(1)}, u32[]{:S(2)}, u32[]{:S(2)}) collective-permute-start(f32[192,128]{1,0:T(8,128)S(1)} %get-tuple-element.21.part_ref), channel_id=1, source_target_pairs={{0,1},{1,0},{2,3},{3,2},{4,5},{5,4},{6,7},{7,6},{8,9},{9,8},{10,11... | collective-permute-start | bytes 294920 | tf_op jit(solution)/shard_map/ppermute | solution.py:453
  8.2 0.0 collective-permute-start.2
  8.2 3.8 %collective-permute-done.2.edge_other_ref = f32[48,128]{1,0:T(8,128)S(1)} collective-permute-done((f32[48,128]{1,0:T(8,128)S(1)}, f32[48,128]{1,0:T(8,128)S(1)}, u32[]{:S(2)}, u32[]{:S(2)}) %collective-permute-start.2) | collective-permute-done | bytes 24608 | tf_op jit(solution)/shard_map/ppermute | solution.py:453
  12.0 0.0 collective-permute-done.other_ref
  12.0 0.0 collective-permute-done.3.q_edge_ref.edge_ref
  12.0 0.1 shard_map.70
  12.1 1.9 %collective-permute-start.4 = (f32[24,640]{1,0:T(8,128)S(1)}, f32[24,640]{1,0:T(8,128)S(1)}, u32[]{:S(2)}, u32[]{:S(2)}) collective-permute-start(f32[24,640]{1,0:T(8,128)S(1)} %get-tuple-element.29), channel_id=1, source_target_pairs={{12,0},{0,4},{4,8},{8,12},{13,1},{1,5},{5,9},{9,13},{14,2},{2,6},{... | collective-permute-start | bytes 184328 | tf_op jit(solution)/shard_map/ppermute | solution.py:536
  14.0 2.1 %collective-permute-start.5 = (f32[24,640]{1,0:T(8,128)S(1)}, f32[24,640]{1,0:T(8,128)S(1)}, u32[]{:S(2)}, u32[]{:S(2)}) collective-permute-start(f32[24,640]{1,0:T(8,128)S(1)} %get-tuple-element.30), channel_id=1, source_target_pairs={{0,12},{4,0},{8,4},{12,8},{1,13},{5,1},{9,5},{13,9},{2,14},{6,2},{... | collective-permute-start | bytes 184328 | tf_op jit(solution)/shard_map/ppermute | solution.py:535
  16.1 0.2 shard_map.71.turned_ref
  16.3 2.4 %collective-permute-done.4.above_ref = f32[24,640]{1,0:T(8,128)S(1)} collective-permute-done((f32[24,640]{1,0:T(8,128)S(1)}, f32[24,640]{1,0:T(8,128)S(1)}, u32[]{:S(2)}, u32[]{:S(2)}) %collective-permute-start.4) | collective-permute-done | bytes 61472 | tf_op jit(solution)/shard_map/ppermute | solution.py:536
  18.6 0.3 collective-permute-done.5.below_ref
  18.9 1.4 %shard_map.72 = (f32[192,128]{1,0:T(8,128)S(1)}, f32[48,640]{1,0:T(8,128)S(1)}) custom-call(f32[48,640]{1,0:T(8,128)S(1)} %get-tuple-element.28.sum_ref, f32[24,640]{1,0:T(8,128)S(1)} %collective-permute-done.4.above_ref, f32[24,640]{1,0:T(8,128)S(1)} %collective-permute-done.5.below_ref, f32[48,640]{1,0:T(8,128)S(1)} %get-tuple-element.31.q_ref, ...), custom_call_target="tpu_custom_call" | custom-call | tf_op jit(solution)/shard_map/pallas_call | solution.py:433
  20.2 1.7 %collective-permute-start.6 = (f32[192,128]{1,0:T(8,128)S(1)}, f32[192,128]{1,0:T(8,128)S(1)}, u32[]{:S(2)}, u32[]{:S(2)}) collective-permute-start(f32[192,128]{1,0:T(8,128)S(1)} %get-tuple-element.34.a), channel_id=1, source_target_pairs={{0,1},{1,0},{2,3},{3,2},{4,5},{5,4},{6,7},{7,6},{8,9},{9,8},{10,11... | collective-permute-start | bytes 294920 | tf_op jit(solution)/shard_map/ppermute | solution.py:453
  21.9 3.0 %collective-permute-done.6.b = f32[192,128]{1,0:T(8,128)S(1)} collective-permute-done((f32[192,128]{1,0:T(8,128)S(1)}, f32[192,128]{1,0:T(8,128)S(1)}, u32[]{:S(2)}, u32[]{:S(2)}) %collective-permute-start.6) | collective-permute-done | bytes 98336 | tf_op jit(solution)/shard_map/ppermute | solution.py:453
  24.9 0.1 shard_map.73
  25.0 0.9 %collective-permute-start.7 = (f32[16,640]{1,0:T(8,128)S(1)}, f32[16,640]{1,0:T(8,128)S(1)}, u32[]{:S(2)}, u32[]{:S(2)}) collective-permute-start(f32[16,640]{1,0:T(8,128)S(1)} %get-tuple-element.36), channel_id=1, source_target_pairs={{12,0},{0,4},{4,8},{8,12},{13,1},{1,5},{5,9},{9,13},{14,2},{2,6},{... | collective-permute-start | bytes 122888 | tf_op jit(solution)/shard_map/ppermute | solution.py:536
  25.9 2.9 %collective-permute-start.8 = (f32[16,640]{1,0:T(8,128)S(1)}, f32[16,640]{1,0:T(8,128)S(1)}, u32[]{:S(2)}, u32[]{:S(2)}) collective-permute-start(f32[16,640]{1,0:T(8,128)S(1)} %get-tuple-element.37), channel_id=1, source_target_pairs={{0,12},{4,0},{8,4},{12,8},{1,13},{5,1},{9,5},{13,9},{2,14},{6,2},{... | collective-permute-start | bytes 122888 | tf_op jit(solution)/shard_map/ppermute | solution.py:535
  28.8 2.0 %collective-permute-done.7.above_ref = f32[16,640]{1,0:T(8,128)S(1)} collective-permute-done((f32[16,640]{1,0:T(8,128)S(1)}, f32[16,640]{1,0:T(8,128)S(1)}, u32[]{:S(2)}, u32[]{:S(2)}) %collective-permute-start.7) | collective-permute-done | bytes 40992 | tf_op jit(solution)/shard_map/ppermute | solution.py:536
  30.8 1.5 %shard_map.74 = (f32[3,16,512]{2,1,0:T(8,128)}, f32[6,32,512]{2,1,0:T(8,128)}) custom-call(f32[48,640]{1,0:T(8,128)S(1)} %get-tuple-element.35.sum_ref, f32[16,640]{1,0:T(8,128)S(1)} %collective-permute-done.7.above_ref, f32[16,640]{1,0:T(8,128)S(1)} %collective-permute-done.8.below_ref, f32[48,640]{1,0:T(8,128)S(1)} %get-tuple-element.38.q_ref, ...), custom_call_target="tpu_custom_call" | custom-call | tf_op jit(solution)/shard_map/pallas_call | solution.py:433
  (1 shorter events, 0.0 us)
Async XLA Ops:
  2.5 1.4 %collective-permute-start.1 = (f32[48,128]{1,0:T(8,128)S(1)}, f32[48,128]{1,0:T(8,128)S(1)}, u32[]{:S(2)}, u32[]{:S(2)}) collective-permute-start(f32[48,128]{1,0:T(8,128)S(1)} %get-tuple-element.22), channel_id=1, source_target_pairs={{0,2},{2,0},{1,3},{3,1},{4,6},{6,4},{5,7},{7,5},{8,10},{10,8},{9,1... | collective-permute-start | bytes 73736 | tf_op jit(solution)/shard_map/ppermute | solution.py:453
  5.1 6.9 %collective-permute-start.3 = (f32[240,128]{1,0:T(8,128)S(1)}, f32[240,128]{1,0:T(8,128)S(1)}, u32[]{:S(2)}, u32[]{:S(2)}) collective-permute-start(f32[240,128]{1,0:T(8,128)S(1)} %get-tuple-element.27), channel_id=1, source_target_pairs={{0,2},{2,0},{1,3},{3,1},{4,6},{6,4},{5,7},{7,5},{8,10},{10,8},{9,1... | collective-permute-start | bytes 368648 | tf_op jit(solution)/shard_map/ppermute | solution.py:453
  5.5 6.5 %collective-permute-start = (f32[192,128]{1,0:T(8,128)S(1)}, f32[192,128]{1,0:T(8,128)S(1)}, u32[]{:S(2)}, u32[]{:S(2)}) collective-permute-start(f32[192,128]{1,0:T(8,128)S(1)} %get-tuple-element.21.part_ref), channel_id=1, source_target_pairs={{0,1},{1,0},{2,3},{3,2},{4,5},{5,4},{6,7},{7,6},{8,9},{9,8},{10,11... | collective-permute-start | bytes 294920 | tf_op jit(solution)/shard_map/ppermute | solution.py:453
  8.2 3.8 %collective-permute-start.2 = (f32[48,128]{1,0:T(8,128)S(1)}, f32[48,128]{1,0:T(8,128)S(1)}, u32[]{:S(2)}, u32[]{:S(2)}) collective-permute-start(f32[48,128]{1,0:T(8,128)S(1)} %collective-permute-done.1.edge_ref), channel_id=1, source_target_pairs={{0,1},{1,0},{2,3},{3,2},{4,5},{5,4},{6,7},{7,6},{8,9},{9,8},{10,11... | collective-permute-start | bytes 73736 | tf_op jit(solution)/shard_map/ppermute | solution.py:453
  12.1 6.5 %collective-permute-start.4 = (f32[24,640]{1,0:T(8,128)S(1)}, f32[24,640]{1,0:T(8,128)S(1)}, u32[]{:S(2)}, u32[]{:S(2)}) collective-permute-start(f32[24,640]{1,0:T(8,128)S(1)} %get-tuple-element.29), channel_id=1, source_target_pairs={{12,0},{0,4},{4,8},{8,12},{13,1},{1,5},{5,9},{9,13},{14,2},{2,6},{... | collective-permute-start | bytes 184328 | tf_op jit(solution)/shard_map/ppermute | solution.py:536
  14.0 4.9 %collective-permute-start.5 = (f32[24,640]{1,0:T(8,128)S(1)}, f32[24,640]{1,0:T(8,128)S(1)}, u32[]{:S(2)}, u32[]{:S(2)}) collective-permute-start(f32[24,640]{1,0:T(8,128)S(1)} %get-tuple-element.30), channel_id=1, source_target_pairs={{0,12},{4,0},{8,4},{12,8},{1,13},{5,1},{9,5},{13,9},{2,14},{6,2},{... | collective-permute-start | bytes 184328 | tf_op jit(solution)/shard_map/ppermute | solution.py:535
  20.2 4.7 %collective-permute-start.6 = (f32[192,128]{1,0:T(8,128)S(1)}, f32[192,128]{1,0:T(8,128)S(1)}, u32[]{:S(2)}, u32[]{:S(2)}) collective-permute-start(f32[192,128]{1,0:T(8,128)S(1)} %get-tuple-element.34.a), channel_id=1, source_target_pairs={{0,1},{1,0},{2,3},{3,2},{4,5},{5,4},{6,7},{7,6},{8,9},{9,8},{10,11... | collective-permute-start | bytes 294920 | tf_op jit(solution)/shard_map/ppermute | solution.py:453
  25.0 5.8 %collective-permute-start.7 = (f32[16,640]{1,0:T(8,128)S(1)}, f32[16,640]{1,0:T(8,128)S(1)}, u32[]{:S(2)}, u32[]{:S(2)}) collective-permute-start(f32[16,640]{1,0:T(8,128)S(1)} %get-tuple-element.36), channel_id=1, source_target_pairs={{12,0},{0,4},{4,8},{8,12},{13,1},{1,5},{5,9},{9,13},{14,2},{2,6},{... | collective-permute-start | bytes 122888 | tf_op jit(solution)/shard_map/ppermute | solution.py:536
  25.9 4.9 %collective-permute-start.8 = (f32[16,640]{1,0:T(8,128)S(1)}, f32[16,640]{1,0:T(8,128)S(1)}, u32[]{:S(2)}, u32[]{:S(2)}) collective-permute-start(f32[16,640]{1,0:T(8,128)S(1)} %get-tuple-element.37), channel_id=1, source_target_pairs={{0,12},{4,0},{8,4},{12,8},{1,13},{5,1},{9,5},{13,9},{2,14},{6,2},{... | collective-permute-start | bytes 122888 | tf_op jit(solution)/shard_map/ppermute | solution.py:535
